TPU v7x, 256 devices: a whole 4x4x8 slice. The times are simulated.
256 devices in a mesh: psg: 8 (over z), exp: 32 (over y, x, core).
Axes of the slice: x: 4, y: 4, z: 8, core: 2. Of those that a mesh axis runs over, the one named last changes fastest.
Arguments:
- hidden: bfloat16 [32, 8, 128, 2048], P('exp', 'psg')
- norm_gain: float32 [2048], replicated, may hold values from 0.5 to 2
- router: bfloat16 [2048, 32], replicated, may hold values from -0.125 to 0.125
- gate_proj: bfloat16 [32, 2048, 768], P('exp'), may hold values from -0.125 to 0.125
- up_proj: bfloat16 [32, 2048, 768], P('exp'), may hold values from -0.125 to 0.125
- down_proj: bfloat16 [32, 768, 2048], P('exp'), may hold values from -0.21875 to 0.21875
- final_gain: float32 [2048], replicated, may hold values from 0.5 to 2
- score_vector: bfloat16 [2048], replicated, may hold values from -0.125 to 0.125
- expert_ids: int32 [32, 8, 128, 8], P('exp', 'psg'), may hold values from 0 to 31, as said below
- grades: int32 [32, 8], P('exp'), may hold values from 0 to 4, as said below
- passage_ranks: int32 [32, 8], P('exp'), may hold values from 0 to 7, each once within a row
Outputs:
- loss: float32 [32], P('exp')
- scores: float32 [32, 8], P('exp', 'psg')
- grad_hidden: bfloat16 [32, 8, 128, 2048], P('exp', 'psg')
Inputs may be any that keep to these rules, and one draw needn't show every extreme that they name: `expert_ids`: each token names 8 different experts. Among the tokens of one device each expert is named at most 36 times, and one expert, the same on every device, is named exactly 36 times on every device. `grades`: every query has some passage of grade 4. `passage_ranks`: each rank appears once in each query.
All inputs are finite; a program needn't handle non-finite values.
Results may differ from a plain program's by a relative error of at most 0.0067.
Values may be sent and summed in bfloat16 or wider, within the bound.
A program may use at most 128 MiB of HBM per device.

v0:
```python
import jax
import jax.numpy as jnp
from jax import lax
from jax.experimental import pallas as pl
from jax.experimental.pallas import tpu as pltpu
from jax.sharding import PartitionSpec as P

MESH = pl.DeviceIdType.MESH
EPS = 1e-06
LOSS_SCALE = 256.0
SLOTS = 40
MARK = 36
WAYS = 32
NN = (((1,), (0,)), ((), ()))
NT = (((1,), (1,)), ((), ()))
TN = (((0,), (0,)), ((), ()))

GROUPS = (
    ((0, 0), (1, 0)),
    ((3, 0), (0, 1)),
    ((0, 3), (1, 1)),
    ((1, 3), (3, 1)),
    ((3, 3), (2, 0)),
    ((0, 2), (2, 1)),
    ((2, 3), (1, 2)),
    ((3, 2), (2, 2)),
)


def dot(a, b, dims):
    return lax.dot_general(a, b, dims, preferred_element_type=jnp.float32)


def split3(v):
    hi = v.astype(jnp.bfloat16).astype(jnp.float32)
    rest = v - hi
    mid = rest.astype(jnp.bfloat16).astype(jnp.float32)
    low = rest - mid
    return jnp.concatenate([hi, mid, low], axis=0).astype(jnp.bfloat16)


def kernel(
    hid, ids_t, gain, rout_t, fgain, svec, grades, ranks, wg_hbm, wu_hbm, wd_hbm,
    loss_o, score_o, out_o,
    xbuf, wg, wu, wd, gate_s, rinv, toks, gsend, grecv, own_rank, rk,
    xg, aref, bref, actr, ppart, tsend, trecv, hbuf, h3, nref, zbuf,
    rs, rrecv, gown, acc,
    wsem, ag_s, ag_r, pt_s, pt_r, small_s, small_r, ret_s, ret_r,
):
    tokens, width = hid.shape
    units = wg.shape[1]
    half, quarter = tokens // 2, tokens // 4
    planes = zbuf.shape[0]
    me = lax.axis_index("exp")
    z = lax.axis_index("psg")
    core = lax.rem(me, 2)
    cx = lax.rem(lax.div(me, 2), 4)
    cy = lax.div(me, 8)

    def at(dx, dy, other=0):
        side = (1 - core) if other else core
        return (lax.rem(cy + dy, 4) * 4 + lax.rem(cx + dx, 4)) * 2 + side

    barrier = pltpu.get_barrier_semaphore()

    def greet(i, carry):
        pl.semaphore_signal(
            barrier, inc=1, device_id={"exp": lax.rem(me + i, WAYS)}, device_id_type=MESH
        )
        return carry

    lax.fori_loop(1, WAYS, greet, 0)
    for i in range(1, planes):
        pl.semaphore_signal(
            barrier, inc=1, device_id={"psg": lax.rem(z + i, planes)}, device_id_type=MESH
        )
    loads = [
        pltpu.make_async_copy(wg_hbm, wg, wsem.at[0]),
        pltpu.make_async_copy(wu_hbm, wu, wsem.at[1]),
        pltpu.make_async_copy(wd_hbm, wd, wsem.at[2]),
    ]
    for load in loads:
        load.start()

    toks[...] = jnp.zeros_like(toks)

    def norm_rows(i, carry):
        rows = pl.ds(pl.multiple_of(i * 16, 16), 16)
        h = hid[rows, :].astype(jnp.float32)
        r = lax.rsqrt(jnp.mean(h * h, axis=1, keepdims=True) + EPS)
        rinv[rows, :] = r
        toks[...] += jnp.sum(h, axis=0, keepdims=True)
        xbuf[me, rows, :] = (h * r * gain[...]).astype(jnp.bfloat16)
        return carry

    lax.fori_loop(0, tokens // 16, norm_rows, 0)
    pl.semaphore_wait(barrier, WAYS - 1 + planes - 1)

    pending = []

    def offset(h, du, dv):
        du, dv = du % 4, dv % 4
        return (du, dv) if h == 0 else (dv, du)

    def spot(h, du, dv):
        ox, oy = offset(h, du, dv)
        return oy * 4 + ox

    def rows_of(h, q):
        start = h * half
        if q is None:
            return pl.ds(start, half)
        return pl.ds(start + q * quarter, quarter)

    def send(h, du, dv, q, su, sv):
        block = at(*offset(h, du, dv))
        piece = xbuf.at[block, rows_of(h, q)]
        k = len([1 for kind, _ in pending if kind == 0])
        copy = pltpu.make_async_remote_copy(
            src_ref=piece,
            dst_ref=piece,
            send_sem=ag_s.at[k],
            recv_sem=ag_r.at[h, spot(h, du - su, dv - sv), q or 0],
            device_id={"exp": at(*offset(h, su, sv))},
            device_id_type=MESH,
        )
        copy.start()
        pending.append((0, copy))

    def share(h, du, dv):
        block = at(*offset(h, du, dv))
        piece = xbuf.at[block, rows_of(h, None)]
        k = spot(h, du, dv)
        copy = pltpu.make_async_remote_copy(
            src_ref=piece,
            dst_ref=piece,
            send_sem=pt_s.at[h, k],
            recv_sem=pt_r.at[h, k],
            device_id={"exp": at(0, 0, 1)},
            device_id_type=MESH,
        )
        copy.start()
        pending.append((1, copy))

    def arrive(h, du, dv, q):
        block = at(*offset(h, du, dv))
        piece = xbuf.at[block, rows_of(h, q)]
        pltpu.make_async_copy(piece, piece, ag_r.at[h, spot(h, du, dv), q or 0]).wait()

    for h in (0, 1):
        send(h, 0, 0, None, 1, 0)
        send(h, 0, 0, None, 3, 0)
    for h in (0, 1):
        send(h, 0, 0, None, 0, 1)
        send(h, 0, 0, None, 0, 3)
    for h in (0, 1):
        share(h, 0, 0)

    logits = dot(rout_t[...], xbuf[me], NT)
    experts = lax.broadcasted_iota(jnp.int32, (WAYS, tokens), 0)
    picked = ids_t[0:1, :] == experts
    for k in range(1, ids_t.shape[0]):
        picked = jnp.logical_or(picked, ids_t[k : k + 1, :] == experts)
    weights = jnp.where(picked, jnp.exp(logits), 0.0)
    gates = weights / jnp.sum(weights, axis=0, keepdims=True)
    gate_s[...] = gates
    gate_low = gates.astype(jnp.bfloat16).astype(jnp.float32)
    gsend[:, 0, :] = jnp.where(picked, gate_low, -1.0)
    before = (
        lax.broadcasted_iota(jnp.int32, (tokens, tokens), 0)
        < lax.broadcasted_iota(jnp.int32, (tokens, tokens), 1)
    ).astype(jnp.float32).astype(jnp.bfloat16)

    def rank_of(mask):
        place = dot(mask.astype(jnp.float32).astype(jnp.bfloat16), before, NN)
        return jnp.where(mask, place, -1.0)

    own_rank[:, 0, :] = rank_of(picked)

    def to_all(source, target, which):
        def one(i, carry):
            e = lax.rem(me + i, WAYS)
            pltpu.make_async_remote_copy(
                src_ref=source(e),
                dst_ref=target.at[me],
                send_sem=small_s.at[which],
                recv_sem=small_r.at[which],
                device_id={"exp": e},
                device_id_type=MESH,
            ).start()
            return carry

        lax.fori_loop(1, WAYS, one, 0)

    def from_all(target, which, count=WAYS - 1):
        block = target.at[pl.ds(0, count)]
        pltpu.make_async_copy(block, block, small_r.at[which]).wait()

    def sent_all(target, which, count=WAYS - 1):
        block = target.at[pl.ds(0, count)]
        pltpu.make_async_copy(block, block, small_s.at[which]).wait()

    to_all(lambda e: gsend.at[e], grecv, 0)
    grecv[me] = gsend[me]

    for h in (0, 1):
        arrive(h, 3, 0, None)
        send(h, 3, 0, 0, 1, 0)
        send(h, 3, 0, None, 0, 1)
        send(h, 3, 0, None, 0, 3)
        arrive(h, 1, 0, None)
        send(h, 1, 0, 1, 3, 0)
        send(h, 1, 0, None, 0, 1)
        send(h, 1, 0, None, 0, 3)
    for h in (0, 1):
        arrive(h, 0, 3, None)
        send(h, 0, 3, 0, 0, 1)
        arrive(h, 0, 1, None)
        send(h, 0, 1, 1, 0, 3)
    for h in (0, 1):
        for du, dv in ((3, 0), (1, 0), (0, 3), (0, 1)):
            share(h, du, dv)

    from_all(grecv, 0)
    everyone = grecv[:, 0, :]
    rk[:, 0, :] = rank_of(everyone >= 0.0)
    for load in loads[:2]:
        load.wait()
    slot = lax.broadcasted_iota(jnp.int32, (SLOTS, tokens), 0).astype(jnp.float32)
    row_id = lax.broadcasted_iota(jnp.int32, (SLOTS, tokens), 0)

    def sources(group, sign=1):
        return [(at((sign * dx) % 4, (sign * dy) % 4, o), dx, dy, o) for dx, dy in group for o in (0, 1)]

    def forward(group):
        for dx, dy in group:
            for h in (0, 1):
                block = at(dx, dy, 1)
                piece = xbuf.at[block, rows_of(h, None)]
                pltpu.make_async_copy(piece, piece, pt_r.at[h, dy * 4 + dx]).wait()
        members = [s for s, _, _, _ in sources(group)]
        rows, gate_col = [], []
        for s in members:
            hit = slot == rk[s]
            one = jnp.where(hit, 1.0, 0.0)
            rows.append(dot(one.astype(jnp.bfloat16), xbuf[s], NN))
            gate_col.append(jnp.sum(jnp.where(hit, grecv[s], 0.0), axis=1, keepdims=True))
        xg[...] = jnp.concatenate(rows, axis=0).astype(jnp.bfloat16)
        weight = jnp.concatenate(gate_col, axis=0)
        step = min(256, units)

        def tile(n, carry):
            cols = pl.ds(pl.multiple_of(n * step, step), step)
            pre_gate = dot(xg[...], wg[:, cols], NN)
            pre_up = dot(xg[...], wu[:, cols], NN)
            sig = 1.0 / (1.0 + jnp.exp(-pre_gate))
            silu = pre_gate * sig
            slope = sig * (1.0 + pre_gate * (1.0 - sig))
            act = (silu * pre_up).astype(jnp.bfloat16).astype(jnp.float32)
            to_gate = weight * (pre_up * slope)
            to_up = weight * silu
            part = weight * act
            for i, s in enumerate(members):
                span = slice(i * SLOTS, (i + 1) * SLOTS)
                aref[s, :, cols] = to_gate[span]
                bref[s, :, cols] = to_up[span]
                actr[s, :, cols] = act[span]
                ppart[s, :, cols] = jnp.sum(part[span], axis=0, keepdims=True)
            return carry

        lax.fori_loop(0, units // step, tile, 0)

    forward(GROUPS[0])
    for h in (0, 1):
        for q in (0, 1):
            arrive(h, 2, 0, q)
            send(h, 2, 0, q, 0, 1)
            send(h, 2, 0, q, 0, 3)
        share(h, 2, 0)
    forward(GROUPS[1])
    for h in (0, 1):
        for du in (3, 1):
            arrive(h, du, 3, None)
            send(h, du, 3, 0, 0, 1)
            arrive(h, du, 1, None)
            send(h, du, 1, 1, 0, 3)
            share(h, du, 3)
            share(h, du, 1)
    forward(GROUPS[2])
    for h in (0, 1):
        arrive(h, 2, 3, 0)
        send(h, 2, 3, 0, 0, 1)
        arrive(h, 2, 1, 1)
        send(h, 2, 1, 1, 0, 3)
        arrive(h, 2, 3, 1)
        arrive(h, 2, 1, 0)
        share(h, 2, 3)
        share(h, 2, 1)
    forward(GROUPS[3])
    for h in (0, 1):
        arrive(h, 0, 2, 0)
        arrive(h, 0, 2, 1)
        share(h, 0, 2)
    forward(GROUPS[4])
    for h in (0, 1):
        for du in (3, 1):
            arrive(h, du, 2, 0)
            arrive(h, du, 2, 1)
            share(h, du, 2)
    forward(GROUPS[5])
    for h in (0, 1):
        arrive(h, 2, 2, 0)
        arrive(h, 2, 2, 1)
        share(h, 2, 2)
    forward(GROUPS[6])
    forward(GROUPS[7])

    loads[2].wait()
    xg[0 : 3 * WAYS, 0:units] = split3(ppart[:, 0, :])
    wide = min(256, width)

    def term_tile(n, carry):
        cols = pl.ds(pl.multiple_of(n * wide, wide), wide)
        t = dot(xg[0 : 3 * WAYS, 0:units], wd[:, cols], NN)
        tsend[:, 0, cols] = t[0:WAYS] + (t[WAYS : 2 * WAYS] + t[2 * WAYS : 3 * WAYS])
        return carry

    lax.fori_loop(0, width // wide, term_tile, 0)
    to_all(lambda e: tsend.at[e], trecv, 1)
    trecv[me] = tsend[me]
    from_all(trecv, 1)
    pooled = (toks[...] + jnp.sum(trecv[...], axis=0)) / tokens
    inv = lax.rsqrt(jnp.mean(pooled * pooled, axis=1, keepdims=True) + EPS)
    head_dir = fgain[...] * svec[...].astype(jnp.float32)
    score = jnp.sum(pooled * inv * head_dir, axis=1, keepdims=True)
    lean = jnp.mean(pooled * head_dir, axis=1, keepdims=True)
    head = inv * head_dir - pooled * (inv * inv * inv * lean)
    hbuf[me] = head
    zbuf[z] = jnp.broadcast_to(score, (1, zbuf.shape[2]))
    to_all(lambda e: hbuf.at[me], hbuf, 2)
    for i in range(1, planes):
        pltpu.make_async_remote_copy(
            src_ref=zbuf.at[z],
            dst_ref=zbuf.at[z],
            send_sem=small_s.at[3],
            recv_sem=small_r.at[3],
            device_id={"psg": lax.rem(z + i, planes)},
            device_id_type=MESH,
        ).start()
    from_all(hbuf, 2)
    h3[...] = split3(hbuf[:, 0, :])
    step = min(256, units)

    def near_tile(n, carry):
        cols = pl.ds(pl.multiple_of(n * step, step), step)
        t = dot(h3[...], wd[cols, :], NT)
        nref[:, 0, cols] = t[0:WAYS] + (t[WAYS : 2 * WAYS] + t[2 * WAYS : 3 * WAYS])
        return carry

    lax.fori_loop(0, units // step, near_tile, 0)

    back = []

    def backward(group):
        members = sources(group)
        gates_in, ups_in = [], []
        for s, _, _, _ in members:
            near = nref[s]
            gates_in.append(aref[s] * near)
            ups_in.append(bref[s] * near)
        d_gate = jnp.concatenate(gates_in, axis=0).astype(jnp.bfloat16)
        d_up = jnp.concatenate(ups_in, axis=0).astype(jnp.bfloat16)
        xg[:, 0:units] = d_gate
        xg[:, units : 2 * units] = d_up

        def tile(n, carry):
            cols = pl.ds(pl.multiple_of(n * wide, wide), wide)
            g = dot(xg[:, 0:units], wg[cols, :], NT)
            g = g + dot(xg[:, units : 2 * units], wu[cols, :], NT)
            for i, (s, _, _, _) in enumerate(members):
                rs[s, :, cols] = g[i * SLOTS : (i + 1) * SLOTS].astype(jnp.bfloat16)
            return carry

        lax.fori_loop(0, width // wide, tile, 0)
        for s, dx, dy, o in members:
            gg = jnp.sum(actr[s] * nref[s], axis=1, keepdims=True)
            dense = jnp.sum(jnp.where(slot == rk[s], gg, 0.0), axis=0, keepdims=True)
            first = rs[s, :, 0:tokens].astype(jnp.float32)
            rs[s, :, 0:tokens] = jnp.where(row_id == MARK, dense, first).astype(jnp.bfloat16)
        for s, dx, dy, o in members:
            if (dx, dy, o) == (0, 0, 0):
                continue
            k = (dy * 4 + dx) * 2 + o
            mirror = (((-dy) % 4) * 4 + (-dx) % 4) * 2 + o
            copy = pltpu.make_async_remote_copy(
                src_ref=rs.at[s],
                dst_ref=rrecv.at[me],
                send_sem=ret_s.at[k],
                recv_sem=ret_r.at[mirror],
                device_id={"exp": s},
                device_id_type=MESH,
            )
            copy.start()
            back.append(copy)

    for group in reversed(GROUPS):
        backward(group)

    from_all(zbuf, 3, planes - 1)
    eye_r = lax.broadcasted_iota(jnp.int32, (planes, planes), 0)
    eye_c = lax.broadcasted_iota(jnp.int32, (planes, planes), 1)
    eye = eye_r == eye_c

    def column(row):
        return jnp.sum(jnp.where(eye, row, 0.0), axis=1, keepdims=True)

    g_row = grades[...].astype(jnp.float32)
    g_col = column(g_row)
    s_col = zbuf[:, 0, 0:1]
    s_row = jnp.sum(jnp.where(eye, s_col, 0.0), axis=0, keepdims=True)
    ln2 = 0.6931471805599453
    d_row = ln2 / jnp.log(2.0 + ranks[...].astype(jnp.float32))
    d_col = column(d_row)
    worth_row = jnp.exp2(g_row)
    worth_col = column(worth_row)
    ahead = jnp.logical_or(g_row > g_col, jnp.logical_and(g_row == g_col, eye_c < eye_r))
    ideal = jnp.sum(jnp.where(ahead, 1.0, 0.0), axis=1, keepdims=True)
    ideal_gain = jnp.sum((worth_col - 1.0) * ln2 / jnp.log(2.0 + ideal), axis=0, keepdims=True)
    swap = jnp.abs((worth_col - worth_row) * (d_col - d_row)) / ideal_gain
    swap = jnp.where(g_col > g_row, swap, 0.0)
    margin = s_col - s_row
    soft = jnp.maximum(-margin, 0.0) + jnp.log(1.0 + jnp.exp(-jnp.abs(margin)))
    loss_o[0] = jnp.sum(swap * soft)
    pull = swap / (1.0 + jnp.exp(margin))
    d_own = jnp.sum(jnp.where(eye_c == z, pull, 0.0) - jnp.where(eye_r == z, pull, 0.0))
    score_o[0, 0] = jnp.sum(score)
    scale = d_own * (LOSS_SCALE / tokens)

    acc[...] = jnp.zeros_like(acc)
    for group in reversed(GROUPS):
        members = sources(group, -1)
        hits = []
        for e, dx, dy, o in members:
            mx, my = (-dx) % 4, (-dy) % 4
            if (dx, dy, o) == (0, 0, 0):
                rrecv[e] = rs[e]
            else:
                block = rrecv.at[e]
                pltpu.make_async_copy(block, block, ret_r.at[(my * 4 + mx) * 2 + o]).wait()
            hits.append(jnp.where(slot == own_rank[e], 1.0, 0.0))
            mark = rrecv[e, :, 0:tokens].astype(jnp.float32)
            gown[e] = jnp.sum(jnp.where(row_id == MARK, mark, 0.0), axis=0, keepdims=True)
        hit = jnp.concatenate(hits, axis=0).astype(jnp.bfloat16)

        def tile(n, carry):
            cols = pl.ds(pl.multiple_of(n * wide, wide), wide)
            rows = jnp.concatenate(
                [rrecv[e, :, cols].astype(jnp.float32) for e, _, _, _ in members], axis=0
            ).astype(jnp.bfloat16)
            acc[:, cols] += dot(hit, rows, TN)
            return carry

        lax.fori_loop(0, width // wide, tile, 0)

    gate_grad = gown[:, 0, :]
    gates = gate_s[...]
    d_logit = gates * (gate_grad - jnp.sum(gates * gate_grad, axis=0, keepdims=True))
    d_logit = split3(d_logit)
    rout3 = jnp.concatenate([rout_t[...]] * 3, axis=0)
    acc[...] += dot(d_logit, rout3, TN)
    head = hbuf[me]

    def finish(i, carry):
        rows = pl.ds(pl.multiple_of(i * 16, 16), 16)
        h = hid[rows, :].astype(jnp.float32)
        r = rinv[rows, :]
        scaled = acc[rows, :] * gain[...]
        lean = jnp.mean(h * scaled, axis=1, keepdims=True)
        full = r * scaled - h * (r * r * r * lean) + head
        out_o[rows, :] = (full * scale).astype(jnp.bfloat16)
        return carry

    lax.fori_loop(0, tokens // 16, finish, 0)
    for _, copy in pending:
        copy.wait_send()
    for copy in back:
        copy.wait_send()
    sent_all(gsend, 0)
    sent_all(tsend, 1)
    sent_all(hbuf, 2)
    sent_all(zbuf, 3, planes - 1)


def local(
    hidden,
    norm_gain,
    router,
    gate_proj,
    up_proj,
    down_proj,
    final_gain,
    score_vector,
    expert_ids,
    grades,
    passage_ranks,
):
    tokens, width = hidden.shape[2:]
    units = gate_proj.shape[2]
    planes = lax.axis_size("psg")
    f32, bf16 = jnp.float32, jnp.bfloat16
    vmem = pl.BlockSpec(memory_space=pltpu.VMEM)
    any_space = pl.BlockSpec(memory_space=pl.ANY)
    smem = pl.BlockSpec(memory_space=pltpu.SMEM)
    scratch = [
        pltpu.VMEM((WAYS, tokens, width), bf16),
        pltpu.VMEM((width, units), bf16),
        pltpu.VMEM((width, units), bf16),
        pltpu.VMEM((units, width), bf16),
        pltpu.VMEM((WAYS, tokens), f32),
        pltpu.VMEM((tokens, 1), f32),
        pltpu.VMEM((1, width), f32),
        pltpu.VMEM((WAYS, 1, tokens), f32),
        pltpu.VMEM((WAYS, 1, tokens), f32),
        pltpu.VMEM((WAYS, 1, tokens), f32),
        pltpu.VMEM((WAYS, 1, tokens), f32),
        pltpu.VMEM((4 * SLOTS, max(width, 2 * units)), bf16),
        pltpu.VMEM((WAYS, SLOTS, units), f32),
        pltpu.VMEM((WAYS, SLOTS, units), f32),
        pltpu.VMEM((WAYS, SLOTS, units), f32),
        pltpu.VMEM((WAYS, 1, units), f32),
        pltpu.VMEM((WAYS, 1, width), f32),
        pltpu.VMEM((WAYS, 1, width), f32),
        pltpu.VMEM((WAYS, 1, width), f32),
        pltpu.VMEM((3 * WAYS, width), bf16),
        pltpu.VMEM((WAYS, 1, units), f32),
        pltpu.VMEM((planes, 1, tokens), f32),
        pltpu.VMEM((WAYS, SLOTS, width), bf16),
        pltpu.VMEM((WAYS, SLOTS, width), bf16),
        pltpu.VMEM((WAYS, 1, tokens), f32),
        pltpu.VMEM((tokens, width), f32),
        pltpu.SemaphoreType.DMA((3,)),
        pltpu.SemaphoreType.DMA((44,)),
        pltpu.SemaphoreType.DMA((2, 16, 2)),
        pltpu.SemaphoreType.DMA((2, 16)),
        pltpu.SemaphoreType.DMA((2, 16)),
        pltpu.SemaphoreType.DMA((4,)),
        pltpu.SemaphoreType.DMA((4,)),
        pltpu.SemaphoreType.DMA((WAYS,)),
        pltpu.SemaphoreType.DMA((WAYS,)),
    ]
    loss, score, grad = pl.pallas_call(
        kernel,
        out_shape=(
            jax.ShapeDtypeStruct((1,), f32),
            jax.ShapeDtypeStruct((1, 1), f32),
            jax.ShapeDtypeStruct((tokens, width), bf16),
        ),
        in_specs=[vmem] * 8 + [any_space] * 3,
        out_specs=(smem, smem, vmem),
        scratch_shapes=scratch,
        compiler_params=pltpu.CompilerParams(
            collective_id=0, has_side_effects=True, vmem_limit_bytes=62 * 1024 * 1024
        ),
        name="expert_block",
    )(
        hidden.reshape(tokens, width),
        expert_ids.reshape(tokens, -1).T,
        norm_gain.reshape(1, width),
        router.T,
        final_gain.reshape(1, width),
        score_vector.reshape(1, width),
        grades,
        passage_ranks,
        gate_proj[0],
        up_proj[0],
        down_proj[0],
    )
    return loss, score, grad.reshape(1, 1, tokens, width)


def solution(mesh):
    placed = (
        P("exp", "psg", None, None),
        P(),
        P(),
        P("exp", None, None),
        P("exp", None, None),
        P("exp", None, None),
        P(),
        P(),
        P("exp", "psg", None, None),
        P("exp", None),
        P("exp", None),
    )
    return jax.shard_map(
        local,
        mesh=mesh,
        in_specs=placed,
        out_specs=(P("exp"), P("exp", "psg"), P("exp", "psg", None, None)),
        check_vma=False,
    )
```

profile of v0, /device:TPU:5, one launch (start us, length us, event | category | flops | bytes accessed | tf_op | source)
XLA Modules:
  0.0 175.8 jit_solution(10540034594539240712)
XLA Ops:
  0.6 1.3 reshape.28.svec
  1.9 168.6 %expert_block.1 = (f32[1]{0:T(128)}, f32[1,1]{1,0:T(1,128)}, bf16[128,2048]{1,0:T(8,128)(2,1)}) custom-call(bf16[128,2048]{1,0:T(8,128)(2,1)} %bitcast.14, s32[8,128]{1,0:T(8,128)} %bitcast.19, f32[1,2048]{1,0:T(1,128)} %bitcast.17, bf16[32,2048]{1,0:T(8,128)(2,1)} %bitcast.16, f32[1,2048]{1,0:T(1,128)} %bitcast.18, bf16[1,2048]{1,0:T(2,128)(2,1)} %reshape.28.svec, ...), custom_call_target="tpu_custom_call" | custom-call | tf_op jit(solution)/shard_map/expert_block/pallas_call | solution.py:551
  171.7 1.9 %copy.19 = bf16[1,1,128,2048]{3,2,1,0:T(8,128)(2,1)} copy(bf16[1,1,128,2048]{3,2,1,0:T(8,128)(2,1)} %bitcast.15) | data formatting | bytes 1048576
where the time goes:
time: 176 us
  Pallas kernels  169 us (96%)
  between operations  4.1 us (2%)
  local copies, waits for them, and re-layouts  3.17 us (2%)
    pallas_call x1, Pallas kernels, local(): pl.pallas_call(kernel, out_shape=(jax.ShapeDtypeStruct((1,), f32), jax.Sh...  169 us

commit v1 on v0

--- a/solution.py
+++ b/solution.py
@@ -9,7 +9,6 @@
 EPS = 1e-06
 LOSS_SCALE = 256.0
 SLOTS = 40
-MARK = 36
 WAYS = 32
 NN = (((1,), (0,)), ((), ()))
 NT = (((1,), (1,)), ((), ()))
@@ -26,6 +25,27 @@
     ((3, 2), (2, 2)),
 )
 
+BACK_GROUPS = (
+    ((2, 2), (1, 2)),
+    ((2, 1), (3, 2)),
+    ((2, 3), (2, 0)),
+    ((0, 2), (1, 1)),
+    ((1, 3), (3, 1)),
+    ((3, 3), (1, 0)),
+    ((0, 1), (3, 0)),
+    ((0, 3), (0, 0)),
+)
+RELAYS = (
+    ((0, 2, 2), (1, 2, 2), (0, 1, 2)),
+    ((1, 2, 1), (0, 2, 1), (1, 1, 2), (0, 3, 2), (1, 2, 3)),
+    ((0, 2, 3), (1, 3, 2), (1, 0, 2)),
+    ((0, 0, 2), (0, 1, 1), (1, 1, 1), (1, 2, 0), (0, 2, 0)),
+    ((0, 1, 3), (1, 3, 1), (0, 3, 1), (1, 1, 3)),
+    ((0, 3, 3), (1, 3, 3), (0, 1, 0), (1, 0, 1)),
+    ((0, 0, 1), (1, 1, 0), (0, 3, 0), (1, 0, 3)),
+    ((0, 0, 3), (1, 3, 0), (0, 0, 0), (1, 0, 0)),
+)
+
 
 def dot(a, b, dims):
     return lax.dot_general(a, b, dims, preferred_element_type=jnp.float32)
@@ -42,10 +62,10 @@
 def kernel(
     hid, ids_t, gain, rout_t, fgain, svec, grades, ranks, wg_hbm, wu_hbm, wd_hbm,
     loss_o, score_o, out_o,
-    xbuf, wg, wu, wd, gate_s, rinv, toks, gsend, grecv, own_rank, rk,
+    xbuf, wg, wu, wd, gate_s, rinv, toks, gsend, grecv, rk,
     xg, aref, bref, actr, ppart, tsend, trecv, hbuf, h3, nref, zbuf,
-    rs, rrecv, gown, acc,
-    wsem, ag_s, ag_r, pt_s, pt_r, small_s, small_r, ret_s, ret_r,
+    psend, precv, vq, vf, uq, uf, ggsend, gown, acc,
+    wsem, ag_s, ag_r, pt_s, pt_r, small_s, small_r, pr_s, pr_r, tr_s, vq_r, vf_r, uq_r, uf_r,
 ):
     tokens, width = hid.shape
     units = wg.shape[1]
@@ -175,14 +195,12 @@
         place = dot(mask.astype(jnp.float32).astype(jnp.bfloat16), before, NN)
         return jnp.where(mask, place, -1.0)
 
-    own_rank[:, 0, :] = rank_of(picked)
-
-    def to_all(source, target, which):
+    def to_all(source, target, which, put=None):
         def one(i, carry):
             e = lax.rem(me + i, WAYS)
             pltpu.make_async_remote_copy(
                 src_ref=source(e),
-                dst_ref=target.at[me],
+                dst_ref=target.at[me] if put is None else target.at[put],
                 send_sem=small_s.at[which],
                 recv_sem=small_r.at[which],
                 device_id={"exp": e},
@@ -200,8 +218,11 @@
         block = target.at[pl.ds(0, count)]
         pltpu.make_async_copy(block, block, small_s.at[which]).wait()
 
-    to_all(lambda e: gsend.at[e], grecv, 0)
-    grecv[me] = gsend[me]
+    def pair(e):
+        return pl.ds(lax.div(e, 2) * 2, 2)
+
+    to_all(lambda e: gsend.at[pair(e)], grecv, 0, pl.ds(me * 2, 2))
+    grecv[pl.ds(me * 2, 2)] = gsend[pair(me)]
 
     for h in (0, 1):
         arrive(h, 3, 0, None)
@@ -221,13 +242,12 @@
         for du, dv in ((3, 0), (1, 0), (0, 3), (0, 1)):
             share(h, du, dv)
 
-    from_all(grecv, 0)
+    from_all(grecv, 0, 2 * (WAYS - 1))
     everyone = grecv[:, 0, :]
     rk[:, 0, :] = rank_of(everyone >= 0.0)
     for load in loads[:2]:
         load.wait()
     slot = lax.broadcasted_iota(jnp.int32, (SLOTS, tokens), 0).astype(jnp.float32)
-    row_id = lax.broadcasted_iota(jnp.int32, (SLOTS, tokens), 0)
 
     def sources(group, sign=1):
         return [(at((sign * dx) % 4, (sign * dy) % 4, o), dx, dy, o) for dx, dy in group for o in (0, 1)]
@@ -241,10 +261,10 @@
         members = [s for s, _, _, _ in sources(group)]
         rows, gate_col = [], []
         for s in members:
-            hit = slot == rk[s]
+            hit = slot == rk[s * 2 + core]
             one = jnp.where(hit, 1.0, 0.0)
             rows.append(dot(one.astype(jnp.bfloat16), xbuf[s], NN))
-            gate_col.append(jnp.sum(jnp.where(hit, grecv[s], 0.0), axis=1, keepdims=True))
+            gate_col.append(jnp.sum(jnp.where(hit, grecv[s * 2 + core], 0.0), axis=1, keepdims=True))
         xg[...] = jnp.concatenate(rows, axis=0).astype(jnp.bfloat16)
         weight = jnp.concatenate(gate_col, axis=0)
         step = min(256, units)
@@ -359,52 +379,166 @@
 
     lax.fori_loop(0, units // step, near_tile, 0)
 
+    for _, copy in pending:
+        copy.wait_send()
     back = []
 
     def backward(group):
         members = sources(group)
-        gates_in, ups_in = [], []
-        for s, _, _, _ in members:
+        for i, (s, dx, dy, o) in enumerate(members):
             near = nref[s]
-            gates_in.append(aref[s] * near)
-            ups_in.append(bref[s] * near)
-        d_gate = jnp.concatenate(gates_in, axis=0).astype(jnp.bfloat16)
-        d_up = jnp.concatenate(ups_in, axis=0).astype(jnp.bfloat16)
-        xg[:, 0:units] = d_gate
-        xg[:, units : 2 * units] = d_up
+            gg = jnp.sum(actr[s] * near, axis=1, keepdims=True)
+            ggsend[s] = jnp.sum(
+                jnp.where(slot == rk[s * 2 + core], gg, 0.0), axis=0, keepdims=True
+            )
+        xg[:, 0:units] = jnp.concatenate(
+            [aref[s] * nref[s] for s, _, _, _ in members], axis=0
+        ).astype(jnp.bfloat16)
+        xg[:, units : 2 * units] = jnp.concatenate(
+            [bref[s] * nref[s] for s, _, _, _ in members], axis=0
+        ).astype(jnp.bfloat16)
 
         def tile(n, carry):
             cols = pl.ds(pl.multiple_of(n * wide, wide), wide)
             g = dot(xg[:, 0:units], wg[cols, :], NT)
             g = g + dot(xg[:, units : 2 * units], wu[cols, :], NT)
-            for i, (s, _, _, _) in enumerate(members):
-                rs[s, :, cols] = g[i * SLOTS : (i + 1) * SLOTS].astype(jnp.bfloat16)
+            for i, (s, dx, dy, o) in enumerate(members):
+                mine = g[i * SLOTS : (i + 1) * SLOTS].astype(jnp.bfloat16)
+                if o:
+                    psend[dy * 4 + dx, :, cols] = mine
+                else:
+                    xbuf[16 + dy * 4 + dx, 0:SLOTS, cols] = mine
             return carry
 
         lax.fori_loop(0, width // wide, tile, 0)
-        for s, dx, dy, o in members:
-            gg = jnp.sum(actr[s] * nref[s], axis=1, keepdims=True)
-            dense = jnp.sum(jnp.where(slot == rk[s], gg, 0.0), axis=0, keepdims=True)
-            first = rs[s, :, 0:tokens].astype(jnp.float32)
-            rs[s, :, 0:tokens] = jnp.where(row_id == MARK, dense, first).astype(jnp.bfloat16)
-        for s, dx, dy, o in members:
-            if (dx, dy, o) == (0, 0, 0):
-                continue
-            k = (dy * 4 + dx) * 2 + o
-            mirror = (((-dy) % 4) * 4 + (-dx) % 4) * 2 + o
+        for dx, dy in group:
+            k = dy * 4 + dx
             copy = pltpu.make_async_remote_copy(
-                src_ref=rs.at[s],
-                dst_ref=rrecv.at[me],
-                send_sem=ret_s.at[k],
-                recv_sem=ret_r.at[mirror],
-                device_id={"exp": s},
+                src_ref=psend.at[k],
+                dst_ref=precv.at[k],
+                send_sem=pr_s.at[k],
+                recv_sem=pr_r.at[k],
+                device_id={"exp": at(0, 0, 1)},
                 device_id_type=MESH,
             )
             copy.start()
             back.append(copy)
 
-    for group in reversed(GROUPS):
+    def gather(group):
+        hits = []
+        for dx, dy in group:
+            k = dy * 4 + dx
+            pltpu.make_async_copy(precv.at[k], precv.at[k], pr_r.at[k]).wait()
+            s = at(dx, dy)
+            hits.append(
+                jnp.concatenate(
+                    [
+                        jnp.where(slot == rk[s * 2 + core], 1.0, 0.0),
+                        jnp.where(slot == rk[s * 2 + 1 - core], 1.0, 0.0),
+                    ],
+                    axis=0,
+                ).astype(jnp.bfloat16)
+            )
+
+        def tile(n, carry):
+            cols = pl.ds(pl.multiple_of(n * wide, wide), wide)
+            for hit, (dx, dy) in zip(hits, group):
+                k = dy * 4 + dx
+                rows = jnp.concatenate(
+                    [
+                        xbuf[16 + k, 0:SLOTS, cols].astype(jnp.float32),
+                        precv[k, :, cols].astype(jnp.float32),
+                    ],
+                    axis=0,
+                ).astype(jnp.bfloat16)
+                xbuf[k, :, cols] = dot(hit, rows, TN).astype(jnp.bfloat16)
+            return carry
+
+        lax.fori_loop(0, width // wide, tile, 0)
+
+    def hand(h, k, q, to, landing, sem):
+        copy = pltpu.make_async_remote_copy(
+            src_ref=xbuf.at[k, rows_of(h, q)],
+            dst_ref=landing,
+            send_sem=tr_s.at[len(hops)],
+            recv_sem=sem,
+            device_id={"exp": to},
+            device_id_type=MESH,
+        )
+        copy.start()
+        hops.append(copy)
+
+    hops = []
+
+    def landed(ref, sem):
+        pltpu.make_async_copy(ref, ref, sem).wait()
+
+    def add(h, k, q, refs):
+        start = h * half + (q or 0) * quarter
+        count = half if q is None else quarter
+
+        def rows16(i, carry):
+            here = pl.ds(pl.multiple_of(start + i * 16, 16), 16)
+            there = pl.ds(pl.multiple_of(i * 16, 16), 16)
+            total = xbuf[k, here, :].astype(jnp.float32)
+            for ref in refs:
+                total = total + ref[there, :].astype(jnp.float32)
+            xbuf[k, here, :] = total.astype(jnp.bfloat16)
+            return carry
+
+        lax.fori_loop(0, count // 16, rows16, 0)
+
+    def relay(h, du, dv):
+        k = spot(h, du, dv)
+        if dv == 2:
+            hand(h, k, 0, at(*offset(h, 0, 1)), vq.at[h, du, 0], vq_r.at[h, du, 0])
+            hand(h, k, 1, at(*offset(h, 0, 3)), vq.at[h, du, 1], vq_r.at[h, du, 1])
+            return
+        if dv in (1, 3):
+            side = 0 if dv == 1 else 1
+            landed(vq.at[h, du, side], vq_r.at[h, du, side])
+            add(h, k, side, [vq.at[h, du, side]])
+            hand(h, k, None, at(*offset(h, 0, dv)), vf.at[h, du, side], vf_r.at[h, du, side])
+            return
+        for side in (0, 1):
+            landed(vf.at[h, du, side], vf_r.at[h, du, side])
+        if du == 0:
+            for side in (0, 1):
+                landed(uf.at[h, side], uf_r.at[h, side])
+
+            def last(i, carry):
+                here = pl.ds(pl.multiple_of(h * half + i * 16, 16), 16)
+                there = pl.ds(pl.multiple_of(i * 16, 16), 16)
+                total = xbuf[k, here, :].astype(jnp.float32)
+                for side in (0, 1):
+                    total = total + vf[h, du, side, there, :].astype(jnp.float32)
+                    total = total + uf[h, side, there, :].astype(jnp.float32)
+                acc[here, :] = total
+                return carry
+
+            lax.fori_loop(0, half // 16, last, 0)
+            return
+        add(h, k, None, [vf.at[h, du, 0], vf.at[h, du, 1]])
+        if du == 2:
+            hand(h, k, 0, at(*offset(h, 1, 0)), uq.at[h, 0], uq_r.at[h, 0])
+            hand(h, k, 1, at(*offset(h, 3, 0)), uq.at[h, 1], uq_r.at[h, 1])
+            return
+        side = 0 if du == 1 else 1
+        landed(uq.at[h, side], uq_r.at[h, side])
+        add(h, k, side, [uq.at[h, side]])
+        hand(h, k, None, at(*offset(h, du, 0)), uf.at[h, side], uf_r.at[h, side])
+
+    for j, group in enumerate(BACK_GROUPS):
         backward(group)
+        if j:
+            gather(BACK_GROUPS[j - 1])
+            for step_of in RELAYS[j - 1]:
+                relay(*step_of)
+    to_all(lambda e: ggsend.at[e], gown, 4)
+    gown[me] = ggsend[me]
+    gather(BACK_GROUPS[-1])
+    for step_of in RELAYS[-1][:2]:
+        relay(*step_of)
 
     from_all(zbuf, 3, planes - 1)
     eye_r = lax.broadcasted_iota(jnp.int32, (planes, planes), 0)
@@ -436,37 +570,14 @@
     score_o[0, 0] = jnp.sum(score)
     scale = d_own * (LOSS_SCALE / tokens)
 
-    acc[...] = jnp.zeros_like(acc)
-    for group in reversed(GROUPS):
-        members = sources(group, -1)
-        hits = []
-        for e, dx, dy, o in members:
-            mx, my = (-dx) % 4, (-dy) % 4
-            if (dx, dy, o) == (0, 0, 0):
-                rrecv[e] = rs[e]
-            else:
-                block = rrecv.at[e]
-                pltpu.make_async_copy(block, block, ret_r.at[(my * 4 + mx) * 2 + o]).wait()
-            hits.append(jnp.where(slot == own_rank[e], 1.0, 0.0))
-            mark = rrecv[e, :, 0:tokens].astype(jnp.float32)
-            gown[e] = jnp.sum(jnp.where(row_id == MARK, mark, 0.0), axis=0, keepdims=True)
-        hit = jnp.concatenate(hits, axis=0).astype(jnp.bfloat16)
-
-        def tile(n, carry):
-            cols = pl.ds(pl.multiple_of(n * wide, wide), wide)
-            rows = jnp.concatenate(
-                [rrecv[e, :, cols].astype(jnp.float32) for e, _, _, _ in members], axis=0
-            ).astype(jnp.bfloat16)
-            acc[:, cols] += dot(hit, rows, TN)
-            return carry
-
-        lax.fori_loop(0, width // wide, tile, 0)
-
+    from_all(gown, 4)
     gate_grad = gown[:, 0, :]
     gates = gate_s[...]
     d_logit = gates * (gate_grad - jnp.sum(gates * gate_grad, axis=0, keepdims=True))
     d_logit = split3(d_logit)
     rout3 = jnp.concatenate([rout_t[...]] * 3, axis=0)
+    for step_of in RELAYS[-1][2:]:
+        relay(*step_of)
     acc[...] += dot(d_logit, rout3, TN)
     head = hbuf[me]
 
@@ -481,14 +592,13 @@
         return carry
 
     lax.fori_loop(0, tokens // 16, finish, 0)
-    for _, copy in pending:
+    for copy in back + hops:
         copy.wait_send()
-    for copy in back:
-        copy.wait_send()
-    sent_all(gsend, 0)
+    sent_all(grecv, 0, 2 * (WAYS - 1))
     sent_all(tsend, 1)
     sent_all(hbuf, 2)
     sent_all(zbuf, 3, planes - 1)
+    sent_all(gown, 4)
 
 
 def local(
@@ -520,9 +630,8 @@
         pltpu.VMEM((tokens, 1), f32),
         pltpu.VMEM((1, width), f32),
         pltpu.VMEM((WAYS, 1, tokens), f32),
-        pltpu.VMEM((WAYS, 1, tokens), f32),
-        pltpu.VMEM((WAYS, 1, tokens), f32),
-        pltpu.VMEM((WAYS, 1, tokens), f32),
+        pltpu.VMEM((2 * WAYS, 1, tokens), f32),
+        pltpu.VMEM((2 * WAYS, 1, tokens), f32),
         pltpu.VMEM((4 * SLOTS, max(width, 2 * units)), bf16),
         pltpu.VMEM((WAYS, SLOTS, units), f32),
         pltpu.VMEM((WAYS, SLOTS, units), f32),
@@ -534,8 +643,13 @@
         pltpu.VMEM((3 * WAYS, width), bf16),
         pltpu.VMEM((WAYS, 1, units), f32),
         pltpu.VMEM((planes, 1, tokens), f32),
-        pltpu.VMEM((WAYS, SLOTS, width), bf16),
-        pltpu.VMEM((WAYS, SLOTS, width), bf16),
+        pltpu.VMEM((16, SLOTS, width), bf16),
+        pltpu.VMEM((16, SLOTS, width), bf16),
+        pltpu.VMEM((2, 4, 2, tokens // 4, width), bf16),
+        pltpu.VMEM((2, 4, 2, tokens // 2, width), bf16),
+        pltpu.VMEM((2, 2, tokens // 4, width), bf16),
+        pltpu.VMEM((2, 2, tokens // 2, width), bf16),
+        pltpu.VMEM((WAYS, 1, tokens), f32),
         pltpu.VMEM((WAYS, 1, tokens), f32),
         pltpu.VMEM((tokens, width), f32),
         pltpu.SemaphoreType.DMA((3,)),
@@ -543,10 +657,15 @@
         pltpu.SemaphoreType.DMA((2, 16, 2)),
         pltpu.SemaphoreType.DMA((2, 16)),
         pltpu.SemaphoreType.DMA((2, 16)),
-        pltpu.SemaphoreType.DMA((4,)),
-        pltpu.SemaphoreType.DMA((4,)),
-        pltpu.SemaphoreType.DMA((WAYS,)),
-        pltpu.SemaphoreType.DMA((WAYS,)),
+        pltpu.SemaphoreType.DMA((5,)),
+        pltpu.SemaphoreType.DMA((5,)),
+        pltpu.SemaphoreType.DMA((16,)),
+        pltpu.SemaphoreType.DMA((16,)),
+        pltpu.SemaphoreType.DMA((40,)),
+        pltpu.SemaphoreType.DMA((2, 4, 2)),
+        pltpu.SemaphoreType.DMA((2, 4, 2)),
+        pltpu.SemaphoreType.DMA((2, 2)),
+        pltpu.SemaphoreType.DMA((2, 2)),
     ]
     loss, score, grad = pl.pallas_call(
         kernel,

time: 176 us -> 153 us (0.87)
  Pallas kernels: 169 us -> 144 us
    pallas_call x1, Pallas kernels: 169 us -> 144 us  [local(): pl.pallas_call(kernel, out_shape=(jax.ShapeDtypeStruct((1,), f32), jax.Sh...]
where the time goes in v1:
time: 153 us; the launch traced here: 151 us
  Pallas kernels  144 us (94%)
  between operations  4.1 us (3%)
  local copies, waits for them, and re-layouts  3.17 us (2%)
    pallas_call x1, Pallas kernels, local(): pl.pallas_call(kernel, out_shape=(jax.ShapeDtypeStruct((1,), f32), jax.Sh...  144 us

profile of v1, /device:TPU:5, one launch (start us, length us, event | category | flops | bytes accessed | tf_op | source)
XLA Modules:
  0.0 151.4 jit_solution(13007925348479187314)
XLA Ops:
  0.6 1.3 reshape.28.svec
  1.9 144.1 %expert_block.1 = (f32[1]{0:T(128)}, f32[1,1]{1,0:T(1,128)}, bf16[128,2048]{1,0:T(8,128)(2,1)}) custom-call(bf16[128,2048]{1,0:T(8,128)(2,1)} %bitcast.14, s32[8,128]{1,0:T(8,128)} %bitcast.19, f32[1,2048]{1,0:T(1,128)} %bitcast.17, bf16[32,2048]{1,0:T(8,128)(2,1)} %bitcast.16, f32[1,2048]{1,0:T(1,128)} %bitcast.18, bf16[1,2048]{1,0:T(2,128)(2,1)} %reshape.28.svec, ...), custom_call_target="tpu_custom_call" | custom-call | tf_op jit(solution)/shard_map/expert_block/pallas_call | solution.py:670
  147.2 1.9 %copy.19 = bf16[1,1,128,2048]{3,2,1,0:T(8,128)(2,1)} copy(bf16[1,1,128,2048]{3,2,1,0:T(8,128)(2,1)} %bitcast.15) | data formatting | bytes 1048576

commit v2 on v1

--- a/solution.py
+++ b/solution.py
@@ -15,35 +15,33 @@
 TN = (((0,), (0,)), ((), ()))
 
 GROUPS = (
-    ((0, 0), (1, 0)),
-    ((3, 0), (0, 1)),
-    ((0, 3), (1, 1)),
-    ((1, 3), (3, 1)),
-    ((3, 3), (2, 0)),
-    ((0, 2), (2, 1)),
-    ((2, 3), (1, 2)),
-    ((3, 2), (2, 2)),
+    ((0, 0), (1, 0), (3, 0), (0, 1)),
+    ((0, 3), (1, 1), (1, 3), (3, 1)),
+    ((3, 3), (2, 0), (0, 2)),
+    ((2, 1), (2, 3), (1, 2), (3, 2)),
+    ((2, 2),),
 )
-
-BACK_GROUPS = (
-    ((2, 2), (1, 2)),
-    ((2, 1), (3, 2)),
-    ((2, 3), (2, 0)),
-    ((0, 2), (1, 1)),
-    ((1, 3), (3, 1)),
-    ((3, 3), (1, 0)),
-    ((0, 1), (3, 0)),
-    ((0, 3), (0, 0)),
-)
-RELAYS = (
-    ((0, 2, 2), (1, 2, 2), (0, 1, 2)),
-    ((1, 2, 1), (0, 2, 1), (1, 1, 2), (0, 3, 2), (1, 2, 3)),
-    ((0, 2, 3), (1, 3, 2), (1, 0, 2)),
-    ((0, 0, 2), (0, 1, 1), (1, 1, 1), (1, 2, 0), (0, 2, 0)),
-    ((0, 1, 3), (1, 3, 1), (0, 3, 1), (1, 1, 3)),
-    ((0, 3, 3), (1, 3, 3), (0, 1, 0), (1, 0, 1)),
-    ((0, 0, 1), (1, 1, 0), (0, 3, 0), (1, 0, 3)),
-    ((0, 0, 3), (1, 3, 0), (0, 0, 0), (1, 0, 0)),
+BACK = (
+    (((2, 2), (1, 2)), (), ((0, 2, 2), (1, 2, 2), (0, 1, 2))),
+    (((2, 1), (3, 2)), ((1, 2, 1),), ((1, 1, 2), (0, 3, 2), (0, 2, 1), (1, 2, 3))),
+    (
+        ((2, 3), (2, 0), (0, 2), (1, 1)),
+        (),
+        ((1, 3, 2), (1, 0, 2), (0, 0, 2), (0, 2, 3), (0, 1, 1), (1, 1, 1), (1, 2, 0)),
+    ),
+    (
+        ((1, 3), (3, 1), (3, 3), (0, 0)),
+        ((0, 2, 0),),
+        ((0, 1, 3), (1, 3, 1), (0, 3, 1), (1, 1, 3), (0, 3, 3), (1, 3, 3)),
+    ),
+    (
+        ((1, 0), (0, 1), (3, 0), (0, 3)),
+        (),
+        (
+            (1, 0, 1), (1, 0, 3), (0, 0, 1), (0, 0, 3),
+            (0, 1, 0), (1, 1, 0), (0, 3, 0), (1, 3, 0),
+        ),
+    ),
 )
 
 
@@ -61,9 +59,9 @@
 
 def kernel(
     hid, ids_t, gain, rout_t, fgain, svec, grades, ranks, wg_hbm, wu_hbm, wd_hbm,
-    loss_o, score_o, out_o,
+    stat_o, out_o,
     xbuf, wg, wu, wd, gate_s, rinv, toks, gsend, grecv, rk,
-    xg, aref, bref, actr, ppart, tsend, trecv, hbuf, h3, nref, zbuf,
+    xg, aref, bref, actr, ppart, stage, tsend, trecv, hbuf, headrow, h3, nref, zbuf,
     psend, precv, vq, vf, uq, uf, ggsend, gown, acc,
     wsem, ag_s, ag_r, pt_s, pt_r, small_s, small_r, pr_s, pr_r, tr_s, vq_r, vf_r, uq_r, uf_r,
 ):
@@ -265,14 +263,15 @@
             one = jnp.where(hit, 1.0, 0.0)
             rows.append(dot(one.astype(jnp.bfloat16), xbuf[s], NN))
             gate_col.append(jnp.sum(jnp.where(hit, grecv[s * 2 + core], 0.0), axis=1, keepdims=True))
-        xg[...] = jnp.concatenate(rows, axis=0).astype(jnp.bfloat16)
+        count = len(members) * SLOTS
+        xg[0:count, 0:width] = jnp.concatenate(rows, axis=0).astype(jnp.bfloat16)
         weight = jnp.concatenate(gate_col, axis=0)
         step = min(256, units)
 
         def tile(n, carry):
             cols = pl.ds(pl.multiple_of(n * step, step), step)
-            pre_gate = dot(xg[...], wg[:, cols], NN)
-            pre_up = dot(xg[...], wu[:, cols], NN)
+            pre_gate = dot(xg[0:count, 0:width], wg[:, cols], NN)
+            pre_up = dot(xg[0:count, 0:width], wu[:, cols], NN)
             sig = 1.0 / (1.0 + jnp.exp(-pre_gate))
             silu = pre_gate * sig
             slope = sig * (1.0 + pre_gate * (1.0 - sig))
@@ -297,7 +296,6 @@
             send(h, 2, 0, q, 0, 1)
             send(h, 2, 0, q, 0, 3)
         share(h, 2, 0)
-    forward(GROUPS[1])
     for h in (0, 1):
         for du in (3, 1):
             arrive(h, du, 3, None)
@@ -306,7 +304,7 @@
             send(h, du, 1, 1, 0, 3)
             share(h, du, 3)
             share(h, du, 1)
-    forward(GROUPS[2])
+    forward(GROUPS[1])
     for h in (0, 1):
         arrive(h, 2, 3, 0)
         send(h, 2, 3, 0, 0, 1)
@@ -316,46 +314,52 @@
         arrive(h, 2, 1, 0)
         share(h, 2, 3)
         share(h, 2, 1)
-    forward(GROUPS[3])
     for h in (0, 1):
         arrive(h, 0, 2, 0)
         arrive(h, 0, 2, 1)
         share(h, 0, 2)
-    forward(GROUPS[4])
+    forward(GROUPS[2])
     for h in (0, 1):
         for du in (3, 1):
             arrive(h, du, 2, 0)
             arrive(h, du, 2, 1)
             share(h, du, 2)
-    forward(GROUPS[5])
+    forward(GROUPS[3])
     for h in (0, 1):
         arrive(h, 2, 2, 0)
         arrive(h, 2, 2, 1)
         share(h, 2, 2)
-    forward(GROUPS[6])
-    forward(GROUPS[7])
+    forward(GROUPS[4])
 
     loads[2].wait()
     xg[0 : 3 * WAYS, 0:units] = split3(ppart[:, 0, :])
     wide = min(256, width)
-
-    def term_tile(n, carry):
-        cols = pl.ds(pl.multiple_of(n * wide, wide), wide)
+    lanes = stage.shape[2]
+    blocks = width // lanes
+    for n in range(width // wide):
+        cols = slice(n * wide, (n + 1) * wide)
         t = dot(xg[0 : 3 * WAYS, 0:units], wd[:, cols], NN)
-        tsend[:, 0, cols] = t[0:WAYS] + (t[WAYS : 2 * WAYS] + t[2 * WAYS : 3 * WAYS])
-        return carry
-
-    lax.fori_loop(0, width // wide, term_tile, 0)
+        t = t[0:WAYS] + (t[WAYS : 2 * WAYS] + t[2 * WAYS : 3 * WAYS])
+        for j in range(wide // lanes):
+            stage[:, n * (wide // lanes) + j, :] = t[:, j * lanes : (j + 1) * lanes]
+    tsend[...] = stage[...].astype(jnp.bfloat16)
     to_all(lambda e: tsend.at[e], trecv, 1)
     trecv[me] = tsend[me]
+    own = jnp.concatenate(
+        [toks[:, j * lanes : (j + 1) * lanes] for j in range(blocks)], axis=0
+    )
+    head_dir = fgain[...] * svec[...].astype(jnp.float32)
     from_all(trecv, 1)
-    pooled = (toks[...] + jnp.sum(trecv[...], axis=0)) / tokens
-    inv = lax.rsqrt(jnp.mean(pooled * pooled, axis=1, keepdims=True) + EPS)
-    head_dir = fgain[...] * svec[...].astype(jnp.float32)
-    score = jnp.sum(pooled * inv * head_dir, axis=1, keepdims=True)
-    lean = jnp.mean(pooled * head_dir, axis=1, keepdims=True)
+    pooled = (own + jnp.sum(trecv[...].astype(jnp.float32), axis=0)) / tokens
+
+    def total(v):
+        return jnp.sum(jnp.sum(v, axis=1, keepdims=True), axis=0, keepdims=True)
+
+    inv = lax.rsqrt(total(pooled * pooled) / width + EPS)
+    score = total(pooled * inv * head_dir)
+    lean = total(pooled * head_dir) / width
     head = inv * head_dir - pooled * (inv * inv * inv * lean)
-    hbuf[me] = head
+    hbuf[me] = head.astype(jnp.bfloat16)
     zbuf[z] = jnp.broadcast_to(score, (1, zbuf.shape[2]))
     to_all(lambda e: hbuf.at[me], hbuf, 2)
     for i in range(1, planes):
@@ -367,14 +371,17 @@
             device_id={"psg": lax.rem(z + i, planes)},
             device_id_type=MESH,
         ).start()
+    for j in range(blocks):
+        headrow[:, j * lanes : (j + 1) * lanes] = head[j : j + 1]
     from_all(hbuf, 2)
-    h3[...] = split3(hbuf[:, 0, :])
+    stage[...] = hbuf[...].astype(jnp.float32)
+    for j in range(blocks):
+        h3[:, j * lanes : (j + 1) * lanes] = stage[:, j, :].astype(jnp.bfloat16)
     step = min(256, units)
 
     def near_tile(n, carry):
         cols = pl.ds(pl.multiple_of(n * step, step), step)
-        t = dot(h3[...], wd[cols, :], NT)
-        nref[:, 0, cols] = t[0:WAYS] + (t[WAYS : 2 * WAYS] + t[2 * WAYS : 3 * WAYS])
+        nref[:, 0, cols] = dot(h3[...], wd[cols, :], NT)
         return carry
 
     lax.fori_loop(0, units // step, near_tile, 0)
@@ -391,17 +398,18 @@
             ggsend[s] = jnp.sum(
                 jnp.where(slot == rk[s * 2 + core], gg, 0.0), axis=0, keepdims=True
             )
-        xg[:, 0:units] = jnp.concatenate(
+        count = len(members) * SLOTS
+        xg[0:count, 0:units] = jnp.concatenate(
             [aref[s] * nref[s] for s, _, _, _ in members], axis=0
         ).astype(jnp.bfloat16)
-        xg[:, units : 2 * units] = jnp.concatenate(
+        xg[0:count, units : 2 * units] = jnp.concatenate(
             [bref[s] * nref[s] for s, _, _, _ in members], axis=0
         ).astype(jnp.bfloat16)
 
         def tile(n, carry):
             cols = pl.ds(pl.multiple_of(n * wide, wide), wide)
-            g = dot(xg[:, 0:units], wg[cols, :], NT)
-            g = g + dot(xg[:, units : 2 * units], wu[cols, :], NT)
+            g = dot(xg[0:count, 0:units], wg[cols, :], NT)
+            g = g + dot(xg[0:count, units : 2 * units], wu[cols, :], NT)
             for i, (s, dx, dy, o) in enumerate(members):
                 mine = g[i * SLOTS : (i + 1) * SLOTS].astype(jnp.bfloat16)
                 if o:
@@ -427,31 +435,20 @@
     def gather(group):
         hits = []
         for dx, dy in group:
+            s = at(dx, dy)
+            for r in (s * 2 + core, s * 2 + 1 - core):
+                hits.append(jnp.where(slot == rk[r], 1.0, 0.0).T.astype(jnp.bfloat16))
+        for dx, dy in group:
             k = dy * 4 + dx
             pltpu.make_async_copy(precv.at[k], precv.at[k], pr_r.at[k]).wait()
-            s = at(dx, dy)
-            hits.append(
-                jnp.concatenate(
-                    [
-                        jnp.where(slot == rk[s * 2 + core], 1.0, 0.0),
-                        jnp.where(slot == rk[s * 2 + 1 - core], 1.0, 0.0),
-                    ],
-                    axis=0,
-                ).astype(jnp.bfloat16)
-            )
 
         def tile(n, carry):
             cols = pl.ds(pl.multiple_of(n * wide, wide), wide)
-            for hit, (dx, dy) in zip(hits, group):
+            for i, (dx, dy) in enumerate(group):
                 k = dy * 4 + dx
-                rows = jnp.concatenate(
-                    [
-                        xbuf[16 + k, 0:SLOTS, cols].astype(jnp.float32),
-                        precv[k, :, cols].astype(jnp.float32),
-                    ],
-                    axis=0,
-                ).astype(jnp.bfloat16)
-                xbuf[k, :, cols] = dot(hit, rows, TN).astype(jnp.bfloat16)
+                rows = dot(hits[2 * i], xbuf[16 + k, 0:SLOTS, cols], NN)
+                rows = rows + dot(hits[2 * i + 1], precv[k, :, cols], NN)
+                xbuf[k, :, cols] = rows.astype(jnp.bfloat16)
             return carry
 
         lax.fori_loop(0, width // wide, tile, 0)
@@ -528,17 +525,15 @@
         add(h, k, side, [uq.at[h, side]])
         hand(h, k, None, at(*offset(h, du, 0)), uf.at[h, side], uf_r.at[h, side])
 
-    for j, group in enumerate(BACK_GROUPS):
+    for group, early, late in BACK:
         backward(group)
-        if j:
-            gather(BACK_GROUPS[j - 1])
-            for step_of in RELAYS[j - 1]:
-                relay(*step_of)
+        for step_of in early:
+            relay(*step_of)
+        gather(group)
+        for step_of in late:
+            relay(*step_of)
     to_all(lambda e: ggsend.at[e], gown, 4)
     gown[me] = ggsend[me]
-    gather(BACK_GROUPS[-1])
-    for step_of in RELAYS[-1][:2]:
-        relay(*step_of)
 
     from_all(zbuf, 3, planes - 1)
     eye_r = lax.broadcasted_iota(jnp.int32, (planes, planes), 0)
@@ -564,10 +559,11 @@
     swap = jnp.where(g_col > g_row, swap, 0.0)
     margin = s_col - s_row
     soft = jnp.maximum(-margin, 0.0) + jnp.log(1.0 + jnp.exp(-jnp.abs(margin)))
-    loss_o[0] = jnp.sum(swap * soft)
+    loss = total(swap * soft)
     pull = swap / (1.0 + jnp.exp(margin))
     d_own = jnp.sum(jnp.where(eye_c == z, pull, 0.0) - jnp.where(eye_r == z, pull, 0.0))
-    score_o[0, 0] = jnp.sum(score)
+    spot_of = lax.broadcasted_iota(jnp.int32, stat_o.shape, 1)
+    stat_o[...] = jnp.where(spot_of == 0, loss, score)
     scale = d_own * (LOSS_SCALE / tokens)
 
     from_all(gown, 4)
@@ -576,10 +572,10 @@
     d_logit = gates * (gate_grad - jnp.sum(gates * gate_grad, axis=0, keepdims=True))
     d_logit = split3(d_logit)
     rout3 = jnp.concatenate([rout_t[...]] * 3, axis=0)
-    for step_of in RELAYS[-1][2:]:
-        relay(*step_of)
+    relay(0, 0, 0)
+    relay(1, 0, 0)
     acc[...] += dot(d_logit, rout3, TN)
-    head = hbuf[me]
+    head = headrow[...]
 
     def finish(i, carry):
         rows = pl.ds(pl.multiple_of(i * 16, 16), 16)
@@ -620,7 +616,6 @@
     f32, bf16 = jnp.float32, jnp.bfloat16
     vmem = pl.BlockSpec(memory_space=pltpu.VMEM)
     any_space = pl.BlockSpec(memory_space=pl.ANY)
-    smem = pl.BlockSpec(memory_space=pltpu.SMEM)
     scratch = [
         pltpu.VMEM((WAYS, tokens, width), bf16),
         pltpu.VMEM((width, units), bf16),
@@ -632,15 +627,17 @@
         pltpu.VMEM((WAYS, 1, tokens), f32),
         pltpu.VMEM((2 * WAYS, 1, tokens), f32),
         pltpu.VMEM((2 * WAYS, 1, tokens), f32),
-        pltpu.VMEM((4 * SLOTS, max(width, 2 * units)), bf16),
+        pltpu.VMEM((8 * SLOTS, max(width, 2 * units)), bf16),
         pltpu.VMEM((WAYS, SLOTS, units), f32),
         pltpu.VMEM((WAYS, SLOTS, units), f32),
         pltpu.VMEM((WAYS, SLOTS, units), f32),
         pltpu.VMEM((WAYS, 1, units), f32),
-        pltpu.VMEM((WAYS, 1, width), f32),
-        pltpu.VMEM((WAYS, 1, width), f32),
-        pltpu.VMEM((WAYS, 1, width), f32),
-        pltpu.VMEM((3 * WAYS, width), bf16),
+        pltpu.VMEM((WAYS, width // 128, 128), f32),
+        pltpu.VMEM((WAYS, width // 128, 128), bf16),
+        pltpu.VMEM((WAYS, width // 128, 128), bf16),
+        pltpu.VMEM((WAYS, width // 128, 128), bf16),
+        pltpu.VMEM((1, width), f32),
+        pltpu.VMEM((WAYS, width), bf16),
         pltpu.VMEM((WAYS, 1, units), f32),
         pltpu.VMEM((planes, 1, tokens), f32),
         pltpu.VMEM((16, SLOTS, width), bf16),
@@ -667,15 +664,14 @@
         pltpu.SemaphoreType.DMA((2, 2)),
         pltpu.SemaphoreType.DMA((2, 2)),
     ]
-    loss, score, grad = pl.pallas_call(
+    stat, grad = pl.pallas_call(
         kernel,
         out_shape=(
-            jax.ShapeDtypeStruct((1,), f32),
-            jax.ShapeDtypeStruct((1, 1), f32),
+            jax.ShapeDtypeStruct((1, 128), f32),
             jax.ShapeDtypeStruct((tokens, width), bf16),
         ),
         in_specs=[vmem] * 8 + [any_space] * 3,
-        out_specs=(smem, smem, vmem),
+        out_specs=(vmem, vmem),
         scratch_shapes=scratch,
         compiler_params=pltpu.CompilerParams(
             collective_id=0, has_side_effects=True, vmem_limit_bytes=62 * 1024 * 1024
@@ -686,15 +682,15 @@
         expert_ids.reshape(tokens, -1).T,
         norm_gain.reshape(1, width),
         router.T,
-        final_gain.reshape(1, width),
-        score_vector.reshape(1, width),
+        final_gain.reshape(width // 128, 128),
+        score_vector.reshape(width // 128, 128),
         grades,
         passage_ranks,
         gate_proj[0],
         up_proj[0],
         down_proj[0],
     )
-    return loss, score, grad.reshape(1, 1, tokens, width)
+    return stat[0, 0:1], stat[0:1, 1:2], grad.reshape(1, 1, tokens, width)
 
 
 def solution(mesh):

time: 153 us -> 148 us (0.967)
  between operations: 4.1 us -> 0.64 us
  Pallas kernels: 144 us -> 142 us
    pallas_call x1, Pallas kernels: 144 us -> 142 us  [local(): pl.pallas_call(kernel, out_shape=(jax.ShapeDtypeStruct((1, 128), f32), ja...]
where the time goes in v2:
time: 148 us; the launch traced here: 146 us
  Pallas kernels  142 us (96%)
  local copies, waits for them, and re-layouts  3.21 us (2%)
    pallas_call x1, Pallas kernels, local(): pl.pallas_call(kernel, out_shape=(jax.ShapeDtypeStruct((1, 128), f32), ja...  142 us

profile of v2, /device:TPU:5, one launch (start us, length us, event | category | flops | bytes accessed | tf_op | source)
XLA Modules:
  0.0 146.3 jit_solution(8654761739836230379)
XLA Ops:
  0.6 142.5 %expert_block.1 = (f32[1,128]{1,0:T(1,128)}, bf16[128,2048]{1,0:T(8,128)(2,1)}) custom-call(bf16[128,2048]{1,0:T(8,128)(2,1)} %bitcast.16, s32[8,128]{1,0:T(8,128)} %bitcast.21, f32[1,2048]{1,0:T(1,128)} %bitcast.19, bf16[32,2048]{1,0:T(8,128)(2,1)} %bitcast.18, f32[16,128]{1,0:T(8,128)} %bitcast.20, bf16[16,128]{1,0:T(8,128)(2,1)} %bitcast.22, ...), custom_call_target="tpu_custom_call" | custom-call | tf_op jit(solution)/shard_map/expert_block/pallas_call | solution.py:667
  143.1 1.3 fusion
  144.4 1.9 %copy.15 = bf16[1,1,128,2048]{3,2,1,0:T(8,128)(2,1)} copy(bf16[1,1,128,2048]{3,2,1,0:T(8,128)(2,1)} %bitcast.17) | data formatting | bytes 1048576

commit v3 on v2

--- a/solution.py
+++ b/solution.py
@@ -18,7 +18,8 @@
     ((0, 0), (1, 0), (3, 0), (0, 1)),
     ((0, 3), (1, 1), (1, 3), (3, 1)),
     ((3, 3), (2, 0), (0, 2)),
-    ((2, 1), (2, 3), (1, 2), (3, 2)),
+    ((3, 2), (2, 3)),
+    ((1, 2), (2, 1)),
     ((2, 2),),
 )
 BACK = (
@@ -30,7 +31,7 @@
         ((1, 3, 2), (1, 0, 2), (0, 0, 2), (0, 2, 3), (0, 1, 1), (1, 1, 1), (1, 2, 0)),
     ),
     (
-        ((1, 3), (3, 1), (3, 3), (0, 0)),
+        ((1, 3), (3, 1), (3, 3)),
         ((0, 2, 0),),
         ((0, 1, 3), (1, 3, 1), (0, 3, 1), (1, 1, 3), (0, 3, 3), (1, 3, 3)),
     ),
@@ -319,17 +320,17 @@
         arrive(h, 0, 2, 1)
         share(h, 0, 2)
     forward(GROUPS[2])
-    for h in (0, 1):
-        for du in (3, 1):
+    for du, group in ((3, GROUPS[3]), (1, GROUPS[4])):
+        for h in (0, 1):
             arrive(h, du, 2, 0)
             arrive(h, du, 2, 1)
             share(h, du, 2)
-    forward(GROUPS[3])
+        forward(group)
     for h in (0, 1):
         arrive(h, 2, 2, 0)
         arrive(h, 2, 2, 1)
         share(h, 2, 2)
-    forward(GROUPS[4])
+    forward(GROUPS[5])
 
     loads[2].wait()
     xg[0 : 3 * WAYS, 0:units] = split3(ppart[:, 0, :])
@@ -389,15 +390,10 @@
     for _, copy in pending:
         copy.wait_send()
     back = []
+    turns = width // wide // 2
 
     def backward(group):
         members = sources(group)
-        for i, (s, dx, dy, o) in enumerate(members):
-            near = nref[s]
-            gg = jnp.sum(actr[s] * near, axis=1, keepdims=True)
-            ggsend[s] = jnp.sum(
-                jnp.where(slot == rk[s * 2 + core], gg, 0.0), axis=0, keepdims=True
-            )
         count = len(members) * SLOTS
         xg[0:count, 0:units] = jnp.concatenate(
             [aref[s] * nref[s] for s, _, _, _ in members], axis=0
@@ -418,19 +414,21 @@
                     xbuf[16 + dy * 4 + dx, 0:SLOTS, cols] = mine
             return carry
 
-        lax.fori_loop(0, width // wide, tile, 0)
-        for dx, dy in group:
-            k = dy * 4 + dx
-            copy = pltpu.make_async_remote_copy(
-                src_ref=psend.at[k],
-                dst_ref=precv.at[k],
-                send_sem=pr_s.at[k],
-                recv_sem=pr_r.at[k],
-                device_id={"exp": at(0, 0, 1)},
-                device_id_type=MESH,
-            )
-            copy.start()
-            back.append(copy)
+        for c in (0, 1):
+            lax.fori_loop(c * turns, (c + 1) * turns, tile, 0)
+            for dx, dy in group:
+                k = dy * 4 + dx
+                cols = pl.ds(c * (width // 2), width // 2)
+                copy = pltpu.make_async_remote_copy(
+                    src_ref=psend.at[k, :, cols],
+                    dst_ref=precv.at[k, :, cols],
+                    send_sem=pr_s.at[c, k],
+                    recv_sem=pr_r.at[c, k],
+                    device_id={"exp": at(0, 0, 1)},
+                    device_id_type=MESH,
+                )
+                copy.start()
+                back.append(copy)
 
     def gather(group):
         hits = []
@@ -438,10 +436,6 @@
             s = at(dx, dy)
             for r in (s * 2 + core, s * 2 + 1 - core):
                 hits.append(jnp.where(slot == rk[r], 1.0, 0.0).T.astype(jnp.bfloat16))
-        for dx, dy in group:
-            k = dy * 4 + dx
-            pltpu.make_async_copy(precv.at[k], precv.at[k], pr_r.at[k]).wait()
-
         def tile(n, carry):
             cols = pl.ds(pl.multiple_of(n * wide, wide), wide)
             for i, (dx, dy) in enumerate(group):
@@ -451,7 +445,12 @@
                 xbuf[k, :, cols] = rows.astype(jnp.bfloat16)
             return carry
 
-        lax.fori_loop(0, width // wide, tile, 0)
+        for c in (0, 1):
+            for dx, dy in group:
+                k = dy * 4 + dx
+                piece = precv.at[k, :, pl.ds(c * (width // 2), width // 2)]
+                pltpu.make_async_copy(piece, piece, pr_r.at[c, k]).wait()
+            lax.fori_loop(c * turns, (c + 1) * turns, tile, 0)
 
     def hand(h, k, q, to, landing, sem):
         copy = pltpu.make_async_remote_copy(
@@ -506,7 +505,7 @@
             def last(i, carry):
                 here = pl.ds(pl.multiple_of(h * half + i * 16, 16), 16)
                 there = pl.ds(pl.multiple_of(i * 16, 16), 16)
-                total = xbuf[k, here, :].astype(jnp.float32)
+                total = acc[here, :] + xbuf[k, here, :].astype(jnp.float32)
                 for side in (0, 1):
                     total = total + vf[h, du, side, there, :].astype(jnp.float32)
                     total = total + uf[h, side, there, :].astype(jnp.float32)
@@ -532,8 +531,19 @@
         gather(group)
         for step_of in late:
             relay(*step_of)
+
+    def gate_gradient(s, carry):
+        gg = jnp.sum(actr[s] * nref[s], axis=1, keepdims=True)
+        ggsend[s] = jnp.sum(
+            jnp.where(slot == rk[s * 2 + core], gg, 0.0), axis=0, keepdims=True
+        )
+        return carry
+
+    lax.fori_loop(0, WAYS, gate_gradient, 0)
     to_all(lambda e: ggsend.at[e], gown, 4)
     gown[me] = ggsend[me]
+    backward(((0, 0),))
+    gather(((0, 0),))
 
     from_all(zbuf, 3, planes - 1)
     eye_r = lax.broadcasted_iota(jnp.int32, (planes, planes), 0)
@@ -572,9 +582,7 @@
     d_logit = gates * (gate_grad - jnp.sum(gates * gate_grad, axis=0, keepdims=True))
     d_logit = split3(d_logit)
     rout3 = jnp.concatenate([rout_t[...]] * 3, axis=0)
-    relay(0, 0, 0)
-    relay(1, 0, 0)
-    acc[...] += dot(d_logit, rout3, TN)
+    acc[...] = dot(d_logit, rout3, TN)
     head = headrow[...]
 
     def finish(i, carry):
@@ -587,7 +595,9 @@
         out_o[rows, :] = (full * scale).astype(jnp.bfloat16)
         return carry
 
-    lax.fori_loop(0, tokens // 16, finish, 0)
+    for h in (0, 1):
+        relay(h, 0, 0)
+        lax.fori_loop(h * half // 16, (h + 1) * half // 16, finish, 0)
     for copy in back + hops:
         copy.wait_send()
     sent_all(grecv, 0, 2 * (WAYS - 1))
@@ -656,8 +666,8 @@
         pltpu.SemaphoreType.DMA((2, 16)),
         pltpu.SemaphoreType.DMA((5,)),
         pltpu.SemaphoreType.DMA((5,)),
-        pltpu.SemaphoreType.DMA((16,)),
-        pltpu.SemaphoreType.DMA((16,)),
+        pltpu.SemaphoreType.DMA((2, 16)),
+        pltpu.SemaphoreType.DMA((2, 16)),
         pltpu.SemaphoreType.DMA((40,)),
         pltpu.SemaphoreType.DMA((2, 4, 2)),
         pltpu.SemaphoreType.DMA((2, 4, 2)),

time: 148 us -> 147 us (level)
  no operation moved by 1% of the time
where the time goes in v3:
time: 147 us; the launch traced here: 145 us
  Pallas kernels  141 us (96%)
  local copies, waits for them, and re-layouts  3.21 us (2%)
    pallas_call x1, Pallas kernels, local(): pl.pallas_call(kernel, out_shape=(jax.ShapeDtypeStruct((1, 128), f32), ja...  141 us

profile of v3, /device:TPU:5, one launch (start us, length us, event | category | flops | bytes accessed | tf_op | source)
XLA Modules:
  0.0 145.3 jit_solution(3016367034539873255)
XLA Ops:
  0.6 141.4 %expert_block.1 = (f32[1,128]{1,0:T(1,128)}, bf16[128,2048]{1,0:T(8,128)(2,1)}) custom-call(bf16[128,2048]{1,0:T(8,128)(2,1)} %bitcast.16, s32[8,128]{1,0:T(8,128)} %bitcast.21, f32[1,2048]{1,0:T(1,128)} %bitcast.19, bf16[32,2048]{1,0:T(8,128)(2,1)} %bitcast.18, f32[16,128]{1,0:T(8,128)} %bitcast.20, bf16[16,128]{1,0:T(8,128)(2,1)} %bitcast.22, ...), custom_call_target="tpu_custom_call" | custom-call | tf_op jit(solution)/shard_map/expert_block/pallas_call | solution.py:677
  142.1 1.3 fusion
  143.4 1.9 %copy.15 = bf16[1,1,128,2048]{3,2,1,0:T(8,128)(2,1)} copy(bf16[1,1,128,2048]{3,2,1,0:T(8,128)(2,1)} %bitcast.17) | data formatting | bytes 1048576

commit v4 on v3

--- a/solution.py
+++ b/solution.py
@@ -45,6 +45,11 @@
     ),
 )
 
+FAR_FIRST = sorted(
+    [(dx, dy, o) for dx in range(4) for dy in range(4) for o in (0, 1) if dx or dy or o],
+    key=lambda d: -min(d[0], 4 - d[0]) - min(d[1], 4 - d[1]),
+)
+
 
 def dot(a, b, dims):
     return lax.dot_general(a, b, dims, preferred_element_type=jnp.float32)
@@ -64,7 +69,7 @@
     xbuf, wg, wu, wd, gate_s, rinv, toks, gsend, grecv, rk,
     xg, aref, bref, actr, ppart, stage, tsend, trecv, hbuf, headrow, h3, nref, zbuf,
     psend, precv, vq, vf, uq, uf, ggsend, gown, acc,
-    wsem, ag_s, ag_r, pt_s, pt_r, small_s, small_r, pr_s, pr_r, tr_s, vq_r, vf_r, uq_r, uf_r,
+    wsem, ag_s, ag_r, pt_s, pt_r, small_s, small_r, pr_s, pr_r, tr_s, vq_r, vf_r, uq_r, uf_r, ready,
 ):
     tokens, width = hid.shape
     units = wg.shape[1]
@@ -81,18 +86,18 @@
         return (lax.rem(cy + dy, 4) * 4 + lax.rem(cx + dx, 4)) * 2 + side
 
     barrier = pltpu.get_barrier_semaphore()
-
-    def greet(i, carry):
-        pl.semaphore_signal(
-            barrier, inc=1, device_id={"exp": lax.rem(me + i, WAYS)}, device_id_type=MESH
-        )
-        return carry
-
-    lax.fori_loop(1, WAYS, greet, 0)
-    for i in range(1, planes):
-        pl.semaphore_signal(
-            barrier, inc=1, device_id={"psg": lax.rem(z + i, planes)}, device_id_type=MESH
-        )
+    beside = [{"exp": at(*d)} for d in ((1, 0), (3, 0), (0, 1), (0, 3), (0, 0, 1))]
+    beside += [{"psg": lax.rem(z + i, planes)} for i in (1, planes - 1)]
+
+    def greet(sem):
+        for device in beside:
+            pl.semaphore_signal(sem, inc=1, device_id=device, device_id_type=MESH)
+
+    def widen(k):
+        greet(ready.at[k])
+        pl.semaphore_wait(ready.at[k], len(beside))
+
+    greet(barrier)
     loads = [
         pltpu.make_async_copy(wg_hbm, wg, wsem.at[0]),
         pltpu.make_async_copy(wu_hbm, wu, wsem.at[1]),
@@ -113,7 +118,7 @@
         return carry
 
     lax.fori_loop(0, tokens // 16, norm_rows, 0)
-    pl.semaphore_wait(barrier, WAYS - 1 + planes - 1)
+    pl.semaphore_wait(barrier, len(beside))
 
     pending = []
 
@@ -195,8 +200,8 @@
         return jnp.where(mask, place, -1.0)
 
     def to_all(source, target, which, put=None):
-        def one(i, carry):
-            e = lax.rem(me + i, WAYS)
+        for dx, dy, o in FAR_FIRST:
+            e = at(dx, dy, o)
             pltpu.make_async_remote_copy(
                 src_ref=source(e),
                 dst_ref=target.at[me] if put is None else target.at[put],
@@ -205,9 +210,6 @@
                 device_id={"exp": e},
                 device_id_type=MESH,
             ).start()
-            return carry
-
-        lax.fori_loop(1, WAYS, one, 0)
 
     def from_all(target, which, count=WAYS - 1):
         block = target.at[pl.ds(0, count)]
@@ -220,8 +222,8 @@
     def pair(e):
         return pl.ds(lax.div(e, 2) * 2, 2)
 
-    to_all(lambda e: gsend.at[pair(e)], grecv, 0, pl.ds(me * 2, 2))
-    grecv[pl.ds(me * 2, 2)] = gsend[pair(me)]
+    widen(0)
+    widen(1)
 
     for h in (0, 1):
         arrive(h, 3, 0, None)
@@ -232,6 +234,10 @@
         send(h, 1, 0, 1, 3, 0)
         send(h, 1, 0, None, 0, 1)
         send(h, 1, 0, None, 0, 3)
+    widen(2)
+    widen(3)
+    to_all(lambda e: gsend.at[pair(e)], grecv, 0, pl.ds(me * 2, 2))
+    grecv[pl.ds(me * 2, 2)] = gsend[pair(me)]
     for h in (0, 1):
         arrive(h, 0, 3, None)
         send(h, 0, 3, 0, 0, 1)
@@ -673,6 +679,7 @@
         pltpu.SemaphoreType.DMA((2, 4, 2)),
         pltpu.SemaphoreType.DMA((2, 2)),
         pltpu.SemaphoreType.DMA((2, 2)),
+        pltpu.SemaphoreType.REGULAR((4,)),
     ]
     stat, grad = pl.pallas_call(
         kernel,

time: 147 us -> 151 us (1.027)
  Pallas kernels: 141 us -> 145 us
    pallas_call x1, Pallas kernels: 141 us -> 145 us  [local(): pl.pallas_call(kernel, out_shape=(jax.ShapeDtypeStruct((1, 128), f32), ja...]
where the time goes in v4:
time: 151 us; the launch traced here: 148 us
  Pallas kernels  145 us (96%)
  local copies, waits for them, and re-layouts  3.21 us (2%)
    pallas_call x1, Pallas kernels, local(): pl.pallas_call(kernel, out_shape=(jax.ShapeDtypeStruct((1, 128), f32), ja...  145 us

profile of v4, /device:TPU:5, one launch (start us, length us, event | category | flops | bytes accessed | tf_op | source)
XLA Modules:
  0.0 148.5 jit_solution(14627551876247165989)
XLA Ops:
  0.6 144.6 %expert_block.1 = (f32[1,128]{1,0:T(1,128)}, bf16[128,2048]{1,0:T(8,128)(2,1)}) custom-call(bf16[128,2048]{1,0:T(8,128)(2,1)} %bitcast.16, s32[8,128]{1,0:T(8,128)} %bitcast.21, f32[1,2048]{1,0:T(1,128)} %bitcast.19, bf16[32,2048]{1,0:T(8,128)(2,1)} %bitcast.18, f32[16,128]{1,0:T(8,128)} %bitcast.20, bf16[16,128]{1,0:T(8,128)(2,1)} %bitcast.22, ...), custom_call_target="tpu_custom_call" | custom-call | tf_op jit(solution)/shard_map/expert_block/pallas_call | solution.py:684
  145.3 1.3 fusion
  146.6 1.9 %copy.15 = bf16[1,1,128,2048]{3,2,1,0:T(8,128)(2,1)} copy(bf16[1,1,128,2048]{3,2,1,0:T(8,128)(2,1)} %bitcast.17) | data formatting | bytes 1048576

commit v5 on v4

--- a/solution.py
+++ b/solution.py
@@ -23,28 +23,32 @@
     ((2, 2),),
 )
 BACK = (
-    (((2, 2), (1, 2)), (), ((0, 2, 2), (1, 2, 2), (0, 1, 2))),
-    (((2, 1), (3, 2)), ((1, 2, 1),), ((1, 1, 2), (0, 3, 2), (0, 2, 1), (1, 2, 3))),
+    (
+        ((2, 2), (1, 2)),
+        (),
+        ((0, 2, 2), (1, 2, 2), (0, 1, 2)),
+    ),
+    (
+        ((2, 1), (3, 2)),
+        (),
+        ((1, 1, 2), (0, 3, 2)),
+    ),
     (
         ((2, 3), (2, 0), (0, 2), (1, 1)),
-        (),
-        ((1, 3, 2), (1, 0, 2), (0, 0, 2), (0, 2, 3), (0, 1, 1), (1, 1, 1), (1, 2, 0)),
+        ((1, 2, 1), (0, 2, 1), (1, 2, 3)),
+        ((1, 3, 2), (1, 0, 2), (0, 0, 2), (0, 2, 3)),
     ),
     (
         ((1, 3), (3, 1), (3, 3)),
-        ((0, 2, 0),),
-        ((0, 1, 3), (1, 3, 1), (0, 3, 1), (1, 1, 3), (0, 3, 3), (1, 3, 3)),
+        ((0, 1, 1), (1, 1, 1), (1, 2, 0)),
+        ((0, 2, 0), (0, 1, 3), (1, 1, 3), (0, 3, 1), (0, 3, 3)),
     ),
     (
         ((1, 0), (0, 1), (3, 0), (0, 3)),
-        (),
-        (
-            (1, 0, 1), (1, 0, 3), (0, 0, 1), (0, 0, 3),
-            (0, 1, 0), (1, 1, 0), (0, 3, 0), (1, 3, 0),
-        ),
+        ((1, 3, 1), (1, 3, 3)),
+        ((1, 0, 1), (1, 0, 3), (0, 0, 1), (0, 0, 3), (0, 1, 0), (1, 1, 0), (0, 3, 0), (1, 3, 0)),
     ),
 )
-
 FAR_FIRST = sorted(
     [(dx, dy, o) for dx in range(4) for dy in range(4) for o in (0, 1) if dx or dy or o],
     key=lambda d: -min(d[0], 4 - d[0]) - min(d[1], 4 - d[1]),
@@ -118,6 +122,26 @@
         return carry
 
     lax.fori_loop(0, tokens // 16, norm_rows, 0)
+
+    logits = dot(rout_t[...], xbuf[me], NT)
+    experts = lax.broadcasted_iota(jnp.int32, (WAYS, tokens), 0)
+    picked = ids_t[0:1, :] == experts
+    for k in range(1, ids_t.shape[0]):
+        picked = jnp.logical_or(picked, ids_t[k : k + 1, :] == experts)
+    weights = jnp.where(picked, jnp.exp(logits), 0.0)
+    gates = weights / jnp.sum(weights, axis=0, keepdims=True)
+    gate_s[...] = gates
+    gate_low = gates.astype(jnp.bfloat16).astype(jnp.float32)
+    gsend[:, 0, :] = jnp.where(picked, gate_low, -1.0)
+    before = (
+        lax.broadcasted_iota(jnp.int32, (tokens, tokens), 0)
+        < lax.broadcasted_iota(jnp.int32, (tokens, tokens), 1)
+    ).astype(jnp.float32).astype(jnp.bfloat16)
+
+    def rank_of(mask):
+        place = dot(mask.astype(jnp.float32).astype(jnp.bfloat16), before, NN)
+        return jnp.where(mask, place, -1.0)
+
     pl.semaphore_wait(barrier, len(beside))
 
     pending = []
@@ -174,30 +198,6 @@
     for h in (0, 1):
         send(h, 0, 0, None, 1, 0)
         send(h, 0, 0, None, 3, 0)
-    for h in (0, 1):
-        send(h, 0, 0, None, 0, 1)
-        send(h, 0, 0, None, 0, 3)
-    for h in (0, 1):
-        share(h, 0, 0)
-
-    logits = dot(rout_t[...], xbuf[me], NT)
-    experts = lax.broadcasted_iota(jnp.int32, (WAYS, tokens), 0)
-    picked = ids_t[0:1, :] == experts
-    for k in range(1, ids_t.shape[0]):
-        picked = jnp.logical_or(picked, ids_t[k : k + 1, :] == experts)
-    weights = jnp.where(picked, jnp.exp(logits), 0.0)
-    gates = weights / jnp.sum(weights, axis=0, keepdims=True)
-    gate_s[...] = gates
-    gate_low = gates.astype(jnp.bfloat16).astype(jnp.float32)
-    gsend[:, 0, :] = jnp.where(picked, gate_low, -1.0)
-    before = (
-        lax.broadcasted_iota(jnp.int32, (tokens, tokens), 0)
-        < lax.broadcasted_iota(jnp.int32, (tokens, tokens), 1)
-    ).astype(jnp.float32).astype(jnp.bfloat16)
-
-    def rank_of(mask):
-        place = dot(mask.astype(jnp.float32).astype(jnp.bfloat16), before, NN)
-        return jnp.where(mask, place, -1.0)
 
     def to_all(source, target, which, put=None):
         for dx, dy, o in FAR_FIRST:
@@ -222,8 +222,15 @@
     def pair(e):
         return pl.ds(lax.div(e, 2) * 2, 2)
 
-    widen(0)
-    widen(1)
+    for k in range(4):
+        widen(k)
+    to_all(lambda e: gsend.at[pair(e)], grecv, 0, pl.ds(me * 2, 2))
+    grecv[pl.ds(me * 2, 2)] = gsend[pair(me)]
+    for h in (0, 1):
+        send(h, 0, 0, None, 0, 1)
+        send(h, 0, 0, None, 0, 3)
+    for h in (0, 1):
+        share(h, 0, 0)
 
     for h in (0, 1):
         arrive(h, 3, 0, None)
@@ -234,10 +241,6 @@
         send(h, 1, 0, 1, 3, 0)
         send(h, 1, 0, None, 0, 1)
         send(h, 1, 0, None, 0, 3)
-    widen(2)
-    widen(3)
-    to_all(lambda e: gsend.at[pair(e)], grecv, 0, pl.ds(me * 2, 2))
-    grecv[pl.ds(me * 2, 2)] = gsend[pair(me)]
     for h in (0, 1):
         arrive(h, 0, 3, None)
         send(h, 0, 3, 0, 0, 1)

time: 151 us -> 144 us (0.954)
  Pallas kernels: 145 us -> 139 us
    pallas_call x1, Pallas kernels: 145 us -> 139 us  [local(): pl.pallas_call(kernel, out_shape=(jax.ShapeDtypeStruct((1, 128), f32), ja...]
where the time goes in v5:
time: 144 us; the launch traced here: 143 us
  Pallas kernels  139 us (97%)
  local copies, waits for them, and re-layouts  3.21 us (2%)
    pallas_call x1, Pallas kernels, local(): pl.pallas_call(kernel, out_shape=(jax.ShapeDtypeStruct((1, 128), f32), ja...  139 us

profile of v5, /device:TPU:5, one launch (start us, length us, event | category | flops | bytes accessed | tf_op | source)
XLA Modules:
  0.0 142.8 jit_solution(3840199827257476114)
XLA Ops:
  0.6 138.9 %expert_block.1 = (f32[1,128]{1,0:T(1,128)}, bf16[128,2048]{1,0:T(8,128)(2,1)}) custom-call(bf16[128,2048]{1,0:T(8,128)(2,1)} %bitcast.16, s32[8,128]{1,0:T(8,128)} %bitcast.21, f32[1,2048]{1,0:T(1,128)} %bitcast.19, bf16[32,2048]{1,0:T(8,128)(2,1)} %bitcast.18, f32[16,128]{1,0:T(8,128)} %bitcast.20, bf16[16,128]{1,0:T(8,128)(2,1)} %bitcast.22, ...), custom_call_target="tpu_custom_call" | custom-call | tf_op jit(solution)/shard_map/expert_block/pallas_call | solution.py:687
  139.6 1.3 fusion
  140.9 1.9 %copy.15 = bf16[1,1,128,2048]{3,2,1,0:T(8,128)(2,1)} copy(bf16[1,1,128,2048]{3,2,1,0:T(8,128)(2,1)} %bitcast.17) | data formatting | bytes 1048576
